TPU v7x, 32 devices: a whole 2x2x4 slice. The times are simulated.
32 devices in a mesh: groups: 2 (over y), strip: 4 (over z), section: 2 (over x), col: 2 (over core).
Axes of the slice: x: 2, y: 2, z: 4, core: 2. Of those that a mesh axis runs over, the one named last changes fastest.
Arguments:
- x_in: float32 [8, 512, 16, 256], P('groups', None, 'strip', 'col'), parts along dimension 0, may hold values from -6 to 6
- w_reduce: float32 [2, 128, 512], P('section'), may hold values from -0.25 to 0.25
- w_spatial: float32 [2, 9, 128, 128], P('section'), may hold values from -0.1875 to 0.1875
- w_expand: float32 [2, 512, 128], P('section'), may hold values from -0.5 to 0.5
- gain_mid: float32 [2, 2, 128], P('section'), may hold values from 0.1 to 1.9
- bias_mid: float32 [2, 2, 128], P('section'), may hold values from -3 to 3
- gain_out: float32 [2, 512], P('section'), may hold values from 0.1 to 1.9
- bias_out: float32 [2, 512], P('section'), may hold values from -3 to 3
Outputs:
- features: float32 [2, 8, 512, 16, 256], P('section', 'groups', None, 'strip', 'col'), parts along dimension 1
There are 2 independent parts, one for each index of `groups`. A program takes and returns all parts, laid end to end along the dimension named above; an argument that names none is the same for every part. Nothing has to cross between parts.
All inputs are finite; a program needn't handle non-finite values.
Results may differ from a plain program's by a relative error of at most 0.00015.
Values sent between devices are 32-bit elements; how exact they have to be, the bound alone decides.
A program may use at most 64 MiB of HBM per device.

v0:
```python
import functools

import jax
import jax.numpy as jnp
from jax import lax
from jax.experimental import pallas as pl
from jax.experimental.pallas import tpu as pltpu
from jax.sharding import PartitionSpec as P

BF = jnp.bfloat16
F32 = jnp.float32


def split(value):
    high = value.astype(BF)
    return high, (value - high.astype(F32)).astype(BF)


def dot(a, b):
    return jnp.dot(a, b, preferred_element_type=F32)


def down_rows(row, size):
    return jnp.transpose(jnp.broadcast_to(row, (size, size)))


def kernel(
    levels, strips, rows,
    x_ref, wr_ref, ws_ref, wx_ref, pp_ref, out_ref,
    cur, wr_all, ws_all, wx_all, pp_all, red, side, halo, relay,
    w_red, w_spa, w_exp, b_red, b_mid, b_out, sa,
    x_sem, own_sem, wsend, wrecv, rsend, rrecv, hsend, hrecv, nsend, nrecv, ysend, yrecv, out_sem,
):
    tiles = x_ref.shape[0]
    chans = x_ref.shape[1] // rows
    cols = x_ref.shape[2]
    mid = wr_ref.shape[0]
    strip = lax.axis_index("strip")
    sec = lax.axis_index("section")
    col = lax.axis_index("col")
    other = {"col": 1 - col}
    srcs = (wr_ref, ws_ref, wx_ref, pp_ref)
    slots = (wr_all, ws_all, wx_all, pp_all)

    def share(kind, level, which):
        if kind == 0:
            return wr_all.at[level, pl.ds(which * (mid // 2), mid // 2), :]
        if kind == 1:
            return ws_all.at[level, :, pl.ds(which * (mid // 2), mid // 2), :]
        if kind == 2:
            return wx_all.at[level, pl.ds(which * (chans // 2), chans // 2), :]
        return pp_all.at[level]

    def remote(src, dst, send, recv, device):
        return pltpu.make_async_remote_copy(
            src_ref=src, dst_ref=dst, send_sem=send, recv_sem=recv,
            device_id=device, device_id_type=pl.DeviceIdType.MESH,
        )

    own = [
        pltpu.make_async_copy(srcs[k], slots[k].at[sec], own_sem.at[k]) for k in range(4)
    ]
    loads = [
        pltpu.make_async_copy(x_ref.at[m], cur.at[m], x_sem.at[m]) for m in range(tiles)
    ]
    for copy in (own[3], own[0], own[1], own[2]):
        copy.start()
    for copy in loads:
        copy.start()

    barrier = pltpu.get_barrier_semaphore()
    pl.semaphore_signal(barrier, inc=1, device_id=other, device_id_type=pl.DeviceIdType.MESH)
    for step in range(1, levels):
        pl.semaphore_signal(
            barrier, inc=1, device_id={"section": lax.rem(sec + step, levels)},
            device_id_type=pl.DeviceIdType.MESH,
        )

    for there, peer in ((strip > 0, strip - 1), (strip < strips - 1, strip + 1)):
        @pl.when(there)
        def _(peer=peer):
            pl.semaphore_signal(
                barrier, inc=1, device_id={"strip": peer}, device_id_type=pl.DeviceIdType.MESH
            )

    peers = levels + jnp.where(strip > 0, 1, 0) + jnp.where(strip < strips - 1, 1, 0)
    pl.semaphore_wait(barrier, peers)

    for k in (3, 0, 1, 2):
        own[k].wait()
        for target in range(1, levels):
            @pl.when(sec < target)
            def _(k=k, target=target):
                part = share(k, sec, col)
                remote(part, part, wsend.at[k, target], wrecv.at[k, sec], {"section": target}).start()

    @pl.when(strip == 0)
    def _():
        halo[:, :, 0] = jnp.zeros(halo.shape[:2] + halo.shape[3:], F32)
        relay[:, :, 0] = jnp.zeros(relay.shape[:2] + relay.shape[3:], F32)

    @pl.when(strip == strips - 1)
    def _():
        halo[:, :, 1] = jnp.zeros(halo.shape[:2] + halo.shape[3:], F32)
        relay[:, :, 1] = jnp.zeros(relay.shape[:2] + relay.shape[3:], F32)

    def relayed(k, level, which):
        part = share(k, level, which)
        return remote(part, part, rsend.at[k, level], rrecv.at[k, level], other)

    def arrive(level, kinds):
        @pl.when(sec > level)
        def _():
            for k in kinds:
                part = share(k, level, col)
                remote(part, part, wsend.at[k, 0], wrecv.at[k, level], other).wait_recv()
                if k < 3:
                    relayed(k, level, col).start()
            for k in kinds:
                if k < 3:
                    relayed(k, level, 1 - col).wait_recv()

    def prepare_reduce(level):
        arrive(level, (3, 0))
        gain = down_rows(pp_all[level, 0:1, :], mid)
        for at in range(chans // mid):
            cut = slice(at * mid, (at + 1) * mid)
            high, low = split(wr_all[level, :, cut] * gain)
            w_red[level, 0:mid, cut] = high
            w_red[level, mid : 2 * mid, cut] = low
        b_red[level] = down_rows(pp_all[level, 2:3, :], mid)

    def prepare_rest(level):
        arrive(level, (1, 2))
        gain = down_rows(pp_all[level, 1:2, :], mid)
        for tap in range(9):
            p, q = tap // 3, tap % 3
            high, low = split(ws_all[level, tap] * gain)
            w_spa[p, 0:mid, q * mid : (q + 1) * mid] = high
            w_spa[p, mid : 2 * mid, q * mid : (q + 1) * mid] = low
        b_mid[...] = down_rows(pp_all[level, 3:4, :], mid)
        count = chans // mid
        for at in range(count):
            cut = slice(at * mid, (at + 1) * mid)
            high, low = split(wx_all[level, cut, :] * down_rows(pp_all[level, 4 + at : 5 + at, :], mid))
            w_exp[cut, 0:mid] = high
            w_exp[cut, mid : 2 * mid] = high
            w_exp[cut, 2 * mid : 3 * mid] = low
            b_out[cut, :] = down_rows(pp_all[level, 4 + count + at : 5 + count + at, :], mid)

    def to_strip(level, m, way):
        return remote(
            red.at[level, m, rows - 1 if way == 0 else 0], halo.at[level, m, way],
            hsend.at[level, m, way], hrecv.at[level, m, way],
            {"strip": strip + 1 if way == 0 else strip - 1},
        )

    def to_side(level, m):
        return remote(red.at[level, m], side.at[level, m], nsend.at[level, m], nrecv.at[level, m], other)

    def pass_on(level, m, way):
        return remote(
            halo.at[level, m, way], relay.at[level, m, way],
            ysend.at[level, m, way], yrecv.at[level, m, way], other,
        )

    has = (strip > 0, strip < strips - 1)

    def reduce_tile(level, m):
        weights = w_red[level]
        bias = b_red[level]
        for pair in range(rows // 2):
            parts = [
                split(cur.at[m][pl.ds(2 * pair + j, chans, stride=rows), :]) for j in range(2)
            ]
            high = jnp.concatenate([part[0] for part in parts], axis=1)
            low = jnp.concatenate([part[1] for part in parts], axis=1)
            both = dot(weights, high)
            total = both[:mid] + both[mid:] + dot(weights[:mid], low)
            for j in range(2):
                red[level, m, 2 * pair + j] = jnp.maximum(total[:, j * cols : (j + 1) * cols] + bias, 0.0)

        @pl.when(has[1])
        def _():
            to_strip(level, m, 0).start()

        @pl.when(has[0])
        def _():
            to_strip(level, m, 1).start()

        to_side(level, m).start()

    def take_halo(level, m):
        for way in range(2):
            @pl.when(has[way])
            def _(way=way):
                to_strip(level, m, way).wait_recv()
                pass_on(level, m, way).start()

    lane = lax.broadcasted_iota(jnp.int32, (mid, cols), 1)
    left_edge = lane == cols - 1
    right_edge = lane == 0
    left_on = jnp.where(col == 1, 1.0, 0.0).astype(F32)
    right_on = jnp.where(col == 0, 1.0, 0.0).astype(F32)

    def finish_tile(level, m):
        to_side(level, m).wait_recv()
        for way in range(2):
            @pl.when(has[way])
            def _(way=way):
                pass_on(level, m, way).wait_recv()
        for at in range(rows + 2):
            if at == 0:
                centre, beside = halo[level, m, 0], relay[level, m, 0]
            elif at == rows + 1:
                centre, beside = halo[level, m, 1], relay[level, m, 1]
            else:
                centre, beside = red[level, m, at - 1], side[level, m, at - 1]
            lanes = slice(at * cols, (at + 1) * cols)
            left = pltpu.roll(jnp.where(left_edge, beside * left_on, centre), 1, 1)
            right = pltpu.roll(jnp.where(right_edge, beside * right_on, centre), cols - 1, 1)
            for q, value in enumerate((left, centre, right)):
                high, low = split(value)
                sa[q * mid : (q + 1) * mid, lanes] = high
                sa[(3 + q) * mid : (4 + q) * mid, lanes] = low
        bias = b_mid[...]
        for pair in range(rows // 2):
            both = jnp.zeros((2 * mid, 2 * cols), F32)
            one = jnp.zeros((mid, 2 * cols), F32)
            for p in range(3):
                lanes = slice((2 * pair + p) * cols, (2 * pair + p + 2) * cols)
                both = both + dot(w_spa[p], sa[0 : 3 * mid, lanes])
                one = one + dot(w_spa[p, 0:mid, :], sa[3 * mid : 6 * mid, lanes])
            total = both[:mid] + both[mid:] + one
            total = jnp.maximum(total + jnp.concatenate([bias, bias], axis=1), 0.0)
            high, low = split(total)
            stack = jnp.concatenate([high, low, high], axis=0)
            grown = dot(w_exp[...], stack)
            for j in range(2):
                at = pl.ds(2 * pair + j, chans, stride=rows)
                cur.at[m][at, :] = jnp.maximum(
                    cur.at[m][at, :] + grown[:, j * cols : (j + 1) * cols] + b_out[...], 0.0
                )

    def store(m):
        return pltpu.make_async_copy(cur.at[m], out_ref.at[m], out_sem.at[m])

    prepare_reduce(0)

    @pl.loop(0, tiles)
    def _(m):
        pltpu.make_async_copy(x_ref.at[m], cur.at[m], x_sem.at[m]).wait()
        reduce_tile(0, m)

    for level in range(levels):
        @pl.when(sec >= level)
        def _(level=level):
            prepare_rest(level)
            if level + 1 < levels:
                @pl.when(sec > level)
                def _():
                    prepare_reduce(level + 1)

            take_halo(level, 0)

            @pl.loop(0, tiles)
            def _(m):
                @pl.when(m + 1 < tiles)
                def _():
                    take_halo(level, m + 1)

                finish_tile(level, m)
                if level + 1 < levels:
                    @pl.when(sec > level)
                    def _():
                        reduce_tile(level + 1, m)

                @pl.when(sec == level)
                def _():
                    store(m).start()

            @pl.loop(0, tiles)
            def _(m):
                to_side(level, m).wait_send()
                for way in range(2):
                    @pl.when(has[1 - way])
                    def _(way=way):
                        to_strip(level, m, way).wait_send()

                    @pl.when(has[way])
                    def _(way=way):
                        pass_on(level, m, way).wait_send()

                @pl.when(sec == level)
                def _():
                    store(m).wait()

    for k in range(4):
        for target in range(1, levels):
            @pl.when(sec < target)
            def _(k=k, target=target):
                part = share(k, sec, col)
                remote(part, part, wsend.at[k, target], wrecv.at[k, sec], {"section": target}).wait_send()
        if k < 3:
            for level in range(levels - 1):
                @pl.when(sec > level)
                def _(k=k, level=level):
                    relayed(k, level, col).wait_send()


def on_device(levels, strips, x_in, w_reduce, w_spatial, w_expand, gain_mid, bias_mid, gain_out, bias_out):
    tiles, chans, rows, cols = x_in.shape
    mid = w_reduce.shape[1]
    terms = jnp.concatenate(
        [
            gain_mid[0], bias_mid[0],
            gain_out.reshape(chans // mid, mid), bias_out.reshape(chans // mid, mid),
            jnp.zeros((4, mid), F32),
        ],
        axis=0,
    )
    dma = pltpu.SemaphoreType.DMA
    out = pl.pallas_call(
        functools.partial(kernel, levels, strips, rows),
        out_shape=jax.ShapeDtypeStruct((tiles, chans * rows, cols), F32),
        in_specs=[pl.BlockSpec(memory_space=pl.ANY)] * 5,
        out_specs=pl.BlockSpec(memory_space=pl.ANY),
        scratch_shapes=[
            pltpu.VMEM((tiles, chans * rows, cols), F32),
            pltpu.VMEM((levels, mid, chans), F32),
            pltpu.VMEM((levels, 9, mid, mid), F32),
            pltpu.VMEM((levels, chans, mid), F32),
            pltpu.VMEM((levels,) + terms.shape, F32),
            pltpu.VMEM((levels, tiles, rows, mid, cols), F32),
            pltpu.VMEM((levels, tiles, rows, mid, cols), F32),
            pltpu.VMEM((levels, tiles, 2, mid, cols), F32),
            pltpu.VMEM((levels, tiles, 2, mid, cols), F32),
            pltpu.VMEM((levels, 2 * mid, chans), BF),
            pltpu.VMEM((3, 2 * mid, 3 * mid), BF),
            pltpu.VMEM((chans, 3 * mid), BF),
            pltpu.VMEM((levels, mid, cols), F32),
            pltpu.VMEM((mid, cols), F32),
            pltpu.VMEM((chans, cols), F32),
            pltpu.VMEM((6 * mid, (rows + 2) * cols), BF),
            dma((tiles,)),
            dma((4,)),
            dma((4, levels)),
            dma((4, levels)),
            dma((3, levels)),
            dma((3, levels)),
            dma((levels, tiles, 2)),
            dma((levels, tiles, 2)),
            dma((levels, tiles)),
            dma((levels, tiles)),
            dma((levels, tiles, 2)),
            dma((levels, tiles, 2)),
            dma((tiles,)),
        ],
        compiler_params=pltpu.CompilerParams(
            collective_id=0, has_side_effects=True, vmem_limit_bytes=60 * 1024 * 1024
        ),
        name="blocks",
    )(x_in.reshape(tiles, chans * rows, cols), w_reduce[0], w_spatial[0], w_expand[0], terms)
    return out.reshape(1, tiles, chans, rows, cols)


def solution(mesh):
    in_specs = (
        P("groups", None, "strip", "col"),
        P("section", None, None),
        P("section", None, None, None),
        P("section", None, None),
        P("section", None, None),
        P("section", None, None),
        P("section", None),
        P("section", None),
    )
    out_specs = P("section", "groups", None, "strip", "col")
    return jax.shard_map(
        functools.partial(on_device, mesh.shape["section"], mesh.shape["strip"]),
        mesh=mesh, in_specs=in_specs, out_specs=out_specs, check_vma=False,
    )
```

profile of v0, /device:TPU:19, one launch (start us, length us, event | category | flops | bytes accessed | tf_op | source)
XLA Modules:
  0.0 48.3 jit_solution(7969270029403871171)
XLA Ops:
  0.0 2.6 %concatenate.3.pp_ref = f32[16,128]{1,0:T(8,128)} concatenate(f32[2,128]{1,0:T(2,128)} %bitcast.16, f32[2,128]{1,0:T(2,128)} %bitcast.17, f32[4,128]{1,0:T(4,128)} %bitcast.14, f32[4,128]{1,0:T(4,128)} %bitcast.15, f32[4,128]{1,0:T(4,128)S(1)} %broadcast_in_dim.3), dimensions={0} | concatenate | bytes 16384 | tf_op jit(solution)/shard_map/concatenate | solution.py:314
  2.6 41.2 %blocks.1 = f32[4,2048,128]{2,1,0:T(8,128)} custom-call(f32[4,2048,128]{2,1,0:T(8,128)} %bitcast.10, f32[128,512]{1,0:T(8,128)} %bitcast.12, f32[9,128,128]{2,1,0:T(8,128)} %bitcast.11, f32[512,128]{1,0:T(8,128)} %bitcast.13, f32[16,128]{1,0:T(8,128)} %concatenate.3.pp_ref), custom_call_target="tpu_custom_call" | custom-call | tf_op jit(solution)/shard_map/blocks/pallas_call | solution.py:323
  43.8 4.5 %copy.10 = f32[1,4,512,4,128]{4,3,2,1,0:T(4,128)} copy(f32[1,4,512,4,128]{4,3,2,1,0:T(4,128)} %bitcast.9) | data formatting | bytes 8388608
  (1 shorter events, 0.0 us)
where the time goes:
time: 48.5 us; the launch traced here: 48.3 us
  Pallas kernels  41.2 us (85%)
  local copies, waits for them, and re-layouts  7.07 us (15%)
    pallas_call x1, Pallas kernels, on_device(): pl.pallas_call(functools.partial(kernel, levels, strips, rows), out_shape...  41.2 us
    unnamed x1, local copies, waits for them, and re-layouts  4.47 us
    concatenate x1, local copies, waits for them, and re-layouts, on_device(): jnp.concatenate([gain_mid[0], bias_mid[0], gain_out.reshape(chans // mid,...  2.6 us

commit v1 on v0

--- a/solution.py
+++ b/solution.py
@@ -26,10 +26,10 @@
 
 def kernel(
     levels, strips, rows,
-    x_ref, wr_ref, ws_ref, wx_ref, pp_ref, out_ref,
-    cur, wr_all, ws_all, wx_all, pp_all, red, side, halo, relay,
+    x_ref, wr_ref, ws_ref, wx_ref, gm_ref, bm_ref, go_ref, bo_ref, out_ref,
+    cur, wr_all, ws_all, wx_all, gm_all, bm_all, go_all, bo_all, red, side, halo, relay,
     w_red, w_spa, w_exp, b_red, b_mid, b_out, sa,
-    x_sem, own_sem, wsend, wrecv, rsend, rrecv, hsend, hrecv, nsend, nrecv, ysend, yrecv, out_sem,
+    x_sem, own_sem, wsend, wrecv, rsend, rrecv, gsend, grecv, hsend, hrecv, nsend, nrecv, ysend, yrecv, out_sem,
 ):
     tiles = x_ref.shape[0]
     chans = x_ref.shape[1] // rows
@@ -38,18 +38,27 @@
     strip = lax.axis_index("strip")
     sec = lax.axis_index("section")
     col = lax.axis_index("col")
+    group = lax.axis_index("groups")
     other = {"col": 1 - col}
-    srcs = (wr_ref, ws_ref, wx_ref, pp_ref)
-    slots = (wr_all, ws_all, wx_all, pp_all)
-
-    def share(kind, level, which):
+    across = {"groups": 1 - group}
+    srcs = (wr_ref, ws_ref, wx_ref, gm_ref, bm_ref, go_ref, bo_ref)
+    slots = (wr_all, ws_all, wx_all, gm_all, bm_all, go_all, bo_all)
+    kinds = len(srcs)
+    order = (3, 4, 5, 6, 0, 1, 2)
+
+    def cut(kind, level, parts, which):
         if kind == 0:
-            return wr_all.at[level, pl.ds(which * (mid // 2), mid // 2), :]
+            return wr_all.at[level, pl.ds(which * (mid // parts), mid // parts), :]
         if kind == 1:
-            return ws_all.at[level, :, pl.ds(which * (mid // 2), mid // 2), :]
+            return ws_all.at[level, :, pl.ds(which * (mid // parts), mid // parts), :]
         if kind == 2:
-            return wx_all.at[level, pl.ds(which * (chans // 2), chans // 2), :]
-        return pp_all.at[level]
+            return wx_all.at[level, pl.ds(which * (chans // parts), chans // parts), :]
+        return slots[kind].at[level]
+
+    def share(kind, level):
+        if kind == 0:
+            return cut(kind, level, 2, col)
+        return cut(kind, level, 4, 2 * col + group)
 
     def remote(src, dst, send, recv, device):
         return pltpu.make_async_remote_copy(
@@ -58,18 +67,19 @@
         )
 
     own = [
-        pltpu.make_async_copy(srcs[k], slots[k].at[sec], own_sem.at[k]) for k in range(4)
+        pltpu.make_async_copy(srcs[k], slots[k].at[sec], own_sem.at[k]) for k in range(kinds)
     ]
     loads = [
         pltpu.make_async_copy(x_ref.at[m], cur.at[m], x_sem.at[m]) for m in range(tiles)
     ]
-    for copy in (own[3], own[0], own[1], own[2]):
-        copy.start()
+    for k in order:
+        own[k].start()
     for copy in loads:
         copy.start()
 
     barrier = pltpu.get_barrier_semaphore()
     pl.semaphore_signal(barrier, inc=1, device_id=other, device_id_type=pl.DeviceIdType.MESH)
+    pl.semaphore_signal(barrier, inc=1, device_id=across, device_id_type=pl.DeviceIdType.MESH)
     for step in range(1, levels):
         pl.semaphore_signal(
             barrier, inc=1, device_id={"section": lax.rem(sec + step, levels)},
@@ -83,15 +93,15 @@
                 barrier, inc=1, device_id={"strip": peer}, device_id_type=pl.DeviceIdType.MESH
             )
 
-    peers = levels + jnp.where(strip > 0, 1, 0) + jnp.where(strip < strips - 1, 1, 0)
+    peers = levels + 1 + jnp.where(strip > 0, 1, 0) + jnp.where(strip < strips - 1, 1, 0)
     pl.semaphore_wait(barrier, peers)
 
-    for k in (3, 0, 1, 2):
+    for k in order:
         own[k].wait()
         for target in range(1, levels):
             @pl.when(sec < target)
             def _(k=k, target=target):
-                part = share(k, sec, col)
+                part = share(k, sec)
                 remote(part, part, wsend.at[k, target], wrecv.at[k, sec], {"section": target}).start()
 
     @pl.when(strip == 0)
@@ -105,48 +115,74 @@
         relay[:, :, 1] = jnp.zeros(relay.shape[:2] + relay.shape[3:], F32)
 
     def relayed(k, level, which):
-        part = share(k, level, which)
+        part = cut(k, level, 2, which)
         return remote(part, part, rsend.at[k, level], rrecv.at[k, level], other)
 
-    def arrive(level, kinds):
+    def crossed(k, level, which):
+        part = cut(k, level, 4, 2 * col + which)
+        return remote(part, part, gsend.at[k, level], grecv.at[k, level], across)
+
+    def arrived(k, level):
+        part = share(k, level)
+        remote(part, part, wsend.at[k, 0], wrecv.at[k, level], other).wait_recv()
+
+    def step_one(level, k):
         @pl.when(sec > level)
         def _():
-            for k in kinds:
-                part = share(k, level, col)
-                remote(part, part, wsend.at[k, 0], wrecv.at[k, level], other).wait_recv()
-                if k < 3:
-                    relayed(k, level, col).start()
-            for k in kinds:
-                if k < 3:
-                    relayed(k, level, 1 - col).wait_recv()
+            arrived(k, level)
+            crossed(k, level, group).start()
+
+    def step_two(level, k):
+        @pl.when(sec > level)
+        def _():
+            crossed(k, level, 1 - group).wait_recv()
+            relayed(k, level, col).start()
+
+    def step_three(level, k):
+        @pl.when(sec > level)
+        def _():
+            relayed(k, level, 1 - col).wait_recv()
+
+    def arrive_reduce(level):
+        @pl.when(sec > level)
+        def _():
+            arrived(0, level)
+            relayed(0, level, col).start()
+            for k in range(3, kinds):
+                arrived(k, level)
+            relayed(0, level, 1 - col).wait_recv()
 
     def prepare_reduce(level):
-        arrive(level, (3, 0))
-        gain = down_rows(pp_all[level, 0:1, :], mid)
+        arrive_reduce(level)
+        gain = down_rows(gm_all[level, 0:1, :], mid)
         for at in range(chans // mid):
-            cut = slice(at * mid, (at + 1) * mid)
-            high, low = split(wr_all[level, :, cut] * gain)
-            w_red[level, 0:mid, cut] = high
-            w_red[level, mid : 2 * mid, cut] = low
-        b_red[level] = down_rows(pp_all[level, 2:3, :], mid)
+            chunk = slice(at * mid, (at + 1) * mid)
+            high, low = split(wr_all[level, :, chunk] * gain)
+            w_red[level, 0:mid, chunk] = high
+            w_red[level, mid : 2 * mid, chunk] = low
+        b_red[level] = down_rows(bm_all[level, 0:1, :], mid)
 
     def prepare_rest(level):
-        arrive(level, (1, 2))
-        gain = down_rows(pp_all[level, 1:2, :], mid)
+        if level > 0:
+            for step in (step_one, step_two):
+                step(level, 1)
+                step(level, 2)
+        step_three(level, 1)
+        gain = down_rows(gm_all[level, 1:2, :], mid)
         for tap in range(9):
             p, q = tap // 3, tap % 3
             high, low = split(ws_all[level, tap] * gain)
             w_spa[p, 0:mid, q * mid : (q + 1) * mid] = high
             w_spa[p, mid : 2 * mid, q * mid : (q + 1) * mid] = low
-        b_mid[...] = down_rows(pp_all[level, 3:4, :], mid)
-        count = chans // mid
-        for at in range(count):
-            cut = slice(at * mid, (at + 1) * mid)
-            high, low = split(wx_all[level, cut, :] * down_rows(pp_all[level, 4 + at : 5 + at, :], mid))
-            w_exp[cut, 0:mid] = high
-            w_exp[cut, mid : 2 * mid] = high
-            w_exp[cut, 2 * mid : 3 * mid] = low
-            b_out[cut, :] = down_rows(pp_all[level, 4 + count + at : 5 + count + at, :], mid)
+        b_mid[...] = down_rows(bm_all[level, 1:2, :], mid)
+        step_three(level, 2)
+        for at in range(chans // mid):
+            chunk = slice(at * mid, (at + 1) * mid)
+            high, low = split(wx_all[level, chunk, :] * down_rows(go_all[level, :, chunk], mid))
+            w_exp[chunk, 0:mid] = high
+            w_exp[chunk, mid : 2 * mid] = high
+            w_exp[chunk, 2 * mid : 3 * mid] = low
+            b_out[chunk, :] = down_rows(bo_all[level, :, chunk], mid)
 
     def to_strip(level, m, way):
         return remote(
@@ -246,11 +282,21 @@
         return pltpu.make_async_copy(cur.at[m], out_ref.at[m], out_sem.at[m])
 
     prepare_reduce(0)
+    if levels > 1:
+        step_one(0, 1)
 
     @pl.loop(0, tiles)
     def _(m):
         pltpu.make_async_copy(x_ref.at[m], cur.at[m], x_sem.at[m]).wait()
         reduce_tile(0, m)
+        if levels > 1:
+            @pl.when(m == tiles // 2 - 1)
+            def _():
+                step_one(0, 2)
+                step_two(0, 1)
+
+    if levels > 1:
+        step_two(0, 2)
 
     for level in range(levels):
         @pl.when(sec >= level)
@@ -295,42 +341,49 @@
                 def _():
                     store(m).wait()
 
-    for k in range(4):
+    for k in range(kinds):
         for target in range(1, levels):
             @pl.when(sec < target)
             def _(k=k, target=target):
-                part = share(k, sec, col)
+                part = share(k, sec)
                 remote(part, part, wsend.at[k, target], wrecv.at[k, sec], {"section": target}).wait_send()
         if k < 3:
             for level in range(levels - 1):
                 @pl.when(sec > level)
                 def _(k=k, level=level):
                     relayed(k, level, col).wait_send()
+                    if k > 0:
+                        crossed(k, level, group).wait_send()
+
+
+def emit(in_ref, out_ref, sems):
+    copies = [
+        pltpu.make_async_copy(in_ref.at[m], out_ref.at[m], sems.at[m]) for m in range(in_ref.shape[0])
+    ]
+    for copy in copies:
+        copy.start()
+    for copy in copies:
+        copy.wait()
 
 
 def on_device(levels, strips, x_in, w_reduce, w_spatial, w_expand, gain_mid, bias_mid, gain_out, bias_out):
     tiles, chans, rows, cols = x_in.shape
     mid = w_reduce.shape[1]
-    terms = jnp.concatenate(
-        [
-            gain_mid[0], bias_mid[0],
-            gain_out.reshape(chans // mid, mid), bias_out.reshape(chans // mid, mid),
-            jnp.zeros((4, mid), F32),
-        ],
-        axis=0,
-    )
     dma = pltpu.SemaphoreType.DMA
     out = pl.pallas_call(
         functools.partial(kernel, levels, strips, rows),
         out_shape=jax.ShapeDtypeStruct((tiles, chans * rows, cols), F32),
-        in_specs=[pl.BlockSpec(memory_space=pl.ANY)] * 5,
+        in_specs=[pl.BlockSpec(memory_space=pltpu.HBM)] * 8,
         out_specs=pl.BlockSpec(memory_space=pl.ANY),
         scratch_shapes=[
             pltpu.VMEM((tiles, chans * rows, cols), F32),
             pltpu.VMEM((levels, mid, chans), F32),
             pltpu.VMEM((levels, 9, mid, mid), F32),
             pltpu.VMEM((levels, chans, mid), F32),
-            pltpu.VMEM((levels,) + terms.shape, F32),
+            pltpu.VMEM((levels,) + gain_mid.shape[1:], F32),
+            pltpu.VMEM((levels,) + bias_mid.shape[1:], F32),
+            pltpu.VMEM((levels,) + gain_out.shape, F32),
+            pltpu.VMEM((levels,) + bias_out.shape, F32),
             pltpu.VMEM((levels, tiles, rows, mid, cols), F32),
             pltpu.VMEM((levels, tiles, rows, mid, cols), F32),
             pltpu.VMEM((levels, tiles, 2, mid, cols), F32),
@@ -343,9 +396,11 @@
             pltpu.VMEM((chans, cols), F32),
             pltpu.VMEM((6 * mid, (rows + 2) * cols), BF),
             dma((tiles,)),
-            dma((4,)),
-            dma((4, levels)),
-            dma((4, levels)),
+            dma((7,)),
+            dma((7, levels)),
+            dma((7, levels)),
+            dma((3, levels)),
+            dma((3, levels)),
             dma((3, levels)),
             dma((3, levels)),
             dma((levels, tiles, 2)),
@@ -357,10 +412,19 @@
             dma((tiles,)),
         ],
         compiler_params=pltpu.CompilerParams(
-            collective_id=0, has_side_effects=True, vmem_limit_bytes=60 * 1024 * 1024
+            collective_id=0, has_side_effects=True, vmem_limit_bytes=40 * 1024 * 1024
         ),
         name="blocks",
-    )(x_in.reshape(tiles, chans * rows, cols), w_reduce[0], w_spatial[0], w_expand[0], terms)
+    )(x_in.reshape(tiles, chans * rows, cols), w_reduce[0], w_spatial[0], w_expand[0], gain_mid[0], bias_mid[0], gain_out, bias_out)
+    out = pl.pallas_call(
+        emit,
+        out_shape=jax.ShapeDtypeStruct(out.shape, F32),
+        in_specs=[pl.BlockSpec(memory_space=pltpu.VMEM)],
+        out_specs=pl.BlockSpec(memory_space=pltpu.HBM),
+        scratch_shapes=[dma((tiles,))],
+        compiler_params=pltpu.CompilerParams(vmem_limit_bytes=16 * 1024 * 1024),
+        name="emit",
+    )(out)
     return out.reshape(1, tiles, chans, rows, cols)
 
 

time: 48.5 us -> 52.5 us (1.082)
  Pallas kernels: 41.2 us -> 44.3 us
  local copies, waits for them, and re-layouts: 7.07 us -> 7.87 us
    unnamed x1 -> x16, local copies, waits for them, and re-layouts: 4.47 us -> 7.87 us
    concatenate x1 -> x0, local copies, waits for them, and re-layouts: 2.6 us -> none  [on_device(): jnp.concatenate([gain_mid[0], bias_mid[0], gain_out.reshape(chans // mid,...]
    pallas_call x0 -> x1, Pallas kernels: none -> 2.04 us  [on_device(): pl.pallas_call(emit, out_shape=jax.ShapeDtypeStruct(out.shape, F32), in_s...]
    pallas_call x1, Pallas kernels: 41.2 us -> 42.3 us  [on_device(): pl.pallas_call(functools.partial(kernel, levels, strips, rows), out_shape...]
where the time goes in v1:
time: 52.5 us; the launch traced here: 52.2 us
  Pallas kernels  44.3 us (84%)
  local copies, waits for them, and re-layouts  7.87 us (15%)
    pallas_call x1, Pallas kernels, on_device(): pl.pallas_call(functools.partial(kernel, levels, strips, rows), out_shape...  42.3 us
    unnamed x16, local copies, waits for them, and re-layouts  7.87 us
    pallas_call x1, Pallas kernels, on_device(): pl.pallas_call(emit, out_shape=jax.ShapeDtypeStruct(out.shape, F32), in_s...  2.04 us

profile of v1, /device:TPU:19, one launch (start us, length us, event | category | flops | bytes accessed | tf_op | source)
XLA Modules:
  0.0 52.2 jit_solution(17810560153842229109)
XLA Ops:
  0.0 0.0 copy-start
  0.0 2.2 %copy-done = f32[4,512,4,128]{3,2,1,0:T(4,128)S(1)} copy-done((f32[4,512,4,128]{3,2,1,0:T(4,128)S(1)}, f32[4,512,4,128]{3,2,1,0:T(4,128)}, u32[]{:S(2)}) %copy-start) | copy-done | bytes 4194328
  2.2 0.0 copy-start.1
  2.2 1.1 %copy-done.1 = f32[1,9,128,128]{3,2,1,0:T(8,128)S(1)} copy-done((f32[1,9,128,128]{3,2,1,0:T(8,128)S(1)}, f32[1,9,128,128]{3,2,1,0:T(8,128)}, u32[]{:S(2)}) %copy-start.1) | copy-done | bytes 589848
  3.3 0.0 copy-start.2
  3.3 0.9 %copy-done.2 = f32[1,128,512]{2,1,0:T(8,128)S(1)} copy-done((f32[1,128,512]{2,1,0:T(8,128)S(1)}, f32[1,128,512]{2,1,0:T(8,128)}, u32[]{:S(2)}) %copy-start.2) | copy-done | bytes 262168
  4.2 0.0 copy-start.3
  4.2 0.9 %copy-done.3 = f32[1,512,128]{2,1,0:T(8,128)S(1)} copy-done((f32[1,512,128]{2,1,0:T(8,128)S(1)}, f32[1,512,128]{2,1,0:T(8,128)}, u32[]{:S(2)}) %copy-start.3) | copy-done | bytes 262168
  5.2 0.0 copy-start.4
  5.2 0.7 %copy-done.4 = f32[1,512]{1,0:T(1,128)S(1)} copy-done((f32[1,512]{1,0:T(1,128)S(1)}, f32[1,512]{1,0:T(1,128)}, u32[]{:S(2)}) %copy-start.4) | copy-done | bytes 2072
  5.8 0.0 copy-start.5
  5.8 0.7 %copy-done.5 = f32[1,512]{1,0:T(1,128)S(1)} copy-done((f32[1,512]{1,0:T(1,128)S(1)}, f32[1,512]{1,0:T(1,128)}, u32[]{:S(2)}) %copy-start.5) | copy-done | bytes 2072
  6.5 0.0 copy-start.6
  6.5 0.7 %copy-done.6 = f32[1,2,128]{2,1,0:T(2,128)S(1)} copy-done((f32[1,2,128]{2,1,0:T(2,128)S(1)}, f32[1,2,128]{2,1,0:T(2,128)}, u32[]{:S(2)}) %copy-start.6) | copy-done | bytes 1048
  7.2 0.0 copy-start.7
  7.2 0.7 %copy-done.7 = f32[1,2,128]{2,1,0:T(2,128)S(1)} copy-done((f32[1,2,128]{2,1,0:T(2,128)S(1)}, f32[1,2,128]{2,1,0:T(2,128)}, u32[]{:S(2)}) %copy-start.7) | copy-done | bytes 1048
  7.9 42.3 %blocks.1.in_ref = f32[4,2048,128]{2,1,0:T(8,128)S(1)} custom-call(f32[4,2048,128]{2,1,0:T(8,128)S(1)} %bitcast.7, f32[128,512]{1,0:T(8,128)S(1)} %bitcast.9, f32[9,128,128]{2,1,0:T(8,128)S(1)} %bitcast.8, f32[512,128]{1,0:T(8,128)S(1)} %bitcast.10, f32[2,128]{1,0:T(2,128)S(1)} %bitcast.11, f32[2,128]{1,0:T(2,128)S(1)} %bitcast.12, f32[1,512]{1,0:T(1,128)S(1)} %copy-done.4, ...), custom_call_target="tpu_custom_call" | custom-call | tf_op jit(solution)/shard_map/blocks/pallas_call | solution.py:373
  50.1 2.0 %emit.1 = f32[4,2048,128]{2,1,0:T(8,128)} custom-call(f32[4,2048,128]{2,1,0:T(8,128)S(1)} %blocks.1.in_ref), custom_call_target="tpu_custom_call" | custom-call | tf_op jit(solution)/shard_map/emit/pallas_call | solution.py:419
Async XLA Ops:
  0.0 2.2 %copy-start = (f32[4,512,4,128]{3,2,1,0:T(4,128)S(1)}, f32[4,512,4,128]{3,2,1,0:T(4,128)}, u32[]{:S(2)}) copy-start(f32[4,512,4,128]{3,2,1,0:T(4,128)} %param.8) | copy-start | bytes 12582916
  2.2 1.1 %copy-start.1 = (f32[1,9,128,128]{3,2,1,0:T(8,128)S(1)}, f32[1,9,128,128]{3,2,1,0:T(8,128)}, u32[]{:S(2)}) copy-start(f32[1,9,128,128]{3,2,1,0:T(8,128)} %param.10) | copy-start | bytes 1769476
  3.3 0.9 %copy-start.2 = (f32[1,128,512]{2,1,0:T(8,128)S(1)}, f32[1,128,512]{2,1,0:T(8,128)}, u32[]{:S(2)}) copy-start(f32[1,128,512]{2,1,0:T(8,128)} %param.9) | copy-start | bytes 786436
  4.2 0.9 %copy-start.3 = (f32[1,512,128]{2,1,0:T(8,128)S(1)}, f32[1,512,128]{2,1,0:T(8,128)}, u32[]{:S(2)}) copy-start(f32[1,512,128]{2,1,0:T(8,128)} %param.11) | copy-start | bytes 786436
  5.2 0.7 %copy-start.4 = (f32[1,512]{1,0:T(1,128)S(1)}, f32[1,512]{1,0:T(1,128)}, u32[]{:S(2)}) copy-start(f32[1,512]{1,0:T(1,128)} %go_ref.1) | copy-start | bytes 6148
  5.8 0.7 %copy-start.5 = (f32[1,512]{1,0:T(1,128)S(1)}, f32[1,512]{1,0:T(1,128)}, u32[]{:S(2)}) copy-start(f32[1,512]{1,0:T(1,128)} %bo_ref.1) | copy-start | bytes 6148
  6.5 0.7 %copy-start.6 = (f32[1,2,128]{2,1,0:T(2,128)S(1)}, f32[1,2,128]{2,1,0:T(2,128)}, u32[]{:S(2)}) copy-start(f32[1,2,128]{2,1,0:T(2,128)} %param.12) | copy-start | bytes 3076
  7.2 0.7 %copy-start.7 = (f32[1,2,128]{2,1,0:T(2,128)S(1)}, f32[1,2,128]{2,1,0:T(2,128)}, u32[]{:S(2)}) copy-start(f32[1,2,128]{2,1,0:T(2,128)} %param.13) | copy-start | bytes 3076

commit v2 on v1

--- a/solution.py
+++ b/solution.py
@@ -356,14 +356,8 @@
                         crossed(k, level, group).wait_send()
 
 
-def emit(in_ref, out_ref, sems):
-    copies = [
-        pltpu.make_async_copy(in_ref.at[m], out_ref.at[m], sems.at[m]) for m in range(in_ref.shape[0])
-    ]
-    for copy in copies:
-        copy.start()
-    for copy in copies:
-        copy.wait()
+def emit(in_ref, out_ref):
+    out_ref[...] = in_ref[...]
 
 
 def on_device(levels, strips, x_in, w_reduce, w_spatial, w_expand, gain_mid, bias_mid, gain_out, bias_out):
@@ -373,7 +367,7 @@
     out = pl.pallas_call(
         functools.partial(kernel, levels, strips, rows),
         out_shape=jax.ShapeDtypeStruct((tiles, chans * rows, cols), F32),
-        in_specs=[pl.BlockSpec(memory_space=pltpu.HBM)] * 8,
+        in_specs=[pl.BlockSpec(memory_space=pl.ANY)] * 8,
         out_specs=pl.BlockSpec(memory_space=pl.ANY),
         scratch_shapes=[
             pltpu.VMEM((tiles, chans * rows, cols), F32),
@@ -412,17 +406,18 @@
             dma((tiles,)),
         ],
         compiler_params=pltpu.CompilerParams(
-            collective_id=0, has_side_effects=True, vmem_limit_bytes=40 * 1024 * 1024
+            collective_id=0, has_side_effects=True, vmem_limit_bytes=60 * 1024 * 1024
         ),
         name="blocks",
     )(x_in.reshape(tiles, chans * rows, cols), w_reduce[0], w_spatial[0], w_expand[0], gain_mid[0], bias_mid[0], gain_out, bias_out)
+    half = chans * rows // 2
     out = pl.pallas_call(
         emit,
+        grid=(tiles, 2),
         out_shape=jax.ShapeDtypeStruct(out.shape, F32),
-        in_specs=[pl.BlockSpec(memory_space=pltpu.VMEM)],
-        out_specs=pl.BlockSpec(memory_space=pltpu.HBM),
-        scratch_shapes=[dma((tiles,))],
-        compiler_params=pltpu.CompilerParams(vmem_limit_bytes=16 * 1024 * 1024),
+        in_specs=[pl.BlockSpec((1, half, cols), lambda m, h: (m, h, 0))],
+        out_specs=pl.BlockSpec((1, half, cols), lambda m, h: (m, h, 0)),
+        compiler_params=pltpu.CompilerParams(vmem_limit_bytes=60 * 1024 * 1024),
         name="emit",
     )(out)
     return out.reshape(1, tiles, chans, rows, cols)

time: 52.5 us -> 49.3 us (0.939)
  local copies, waits for them, and re-layouts: 7.87 us -> 0 us
  Pallas kernels: 44.3 us -> 49 us
    unnamed x16 -> x0, local copies, waits for them, and re-layouts: 7.87 us -> none
    pallas_call x1, Pallas kernels: 2.04 us -> 6.6 us  [on_device(): pl.pallas_call(emit, grid=(tiles, 2), out_shape=jax.ShapeDtypeStruct(out....]
where the time goes in v2:
time: 49.3 us; the launch traced here: 49 us
  Pallas kernels  49 us (99%)
    pallas_call x1, Pallas kernels, on_device(): pl.pallas_call(functools.partial(kernel, levels, strips, rows), out_shape...  42.4 us
    pallas_call x1, Pallas kernels, on_device(): pl.pallas_call(emit, grid=(tiles, 2), out_shape=jax.ShapeDtypeStruct(out....  6.6 us

profile of v2, /device:TPU:19, one launch (start us, length us, event | category | flops | bytes accessed | tf_op | source)
XLA Modules:
  0.0 49.0 jit_solution(17844035104612834556)
XLA Ops:
  0.0 42.4 %blocks.1.in_ref = f32[4,2048,128]{2,1,0:T(8,128)} custom-call(f32[4,2048,128]{2,1,0:T(8,128)} %bitcast.7, f32[128,512]{1,0:T(8,128)} %bitcast.9, f32[9,128,128]{2,1,0:T(8,128)} %bitcast.8, f32[512,128]{1,0:T(8,128)} %bitcast.10, f32[2,128]{1,0:T(2,128)} %bitcast.11, f32[2,128]{1,0:T(2,128)} %bitcast.12, f32[1,512]{1,0:T(1,128)} %go_ref.1, f32[1,512]{1,0:T(1,128)} %bo_ref.1), custom_call_target="tpu_custom_call" | custom-call | tf_op jit(solution)/shard_map/blocks/pallas_call | solution.py:367
  42.4 6.6 %emit.1 = f32[4,2048,128]{2,1,0:T(8,128)} custom-call(f32[4,2048,128]{2,1,0:T(8,128)} %blocks.1.in_ref), custom_call_target="tpu_custom_call" | custom-call | tf_op jit(solution)/shard_map/emit/pallas_call | solution.py:414
